TPU v7x, 256 devices: a whole 4x4x8 slice. The times are simulated.
256 devices in a mesh: bag: 16 (over x, y), seq: 16 (over z, core).
Axes of the slice: x: 4, y: 4, z: 8, core: 2. Of those that a mesh axis runs over, the one named last changes fastest.
Arguments:
- text_rows: bfloat16 [32768, 3072], P(('bag', 'seq')), may hold values from -6 to 6
- image_rows: bfloat16 [8192, 3072], P(('bag', 'seq')), may hold values from -6 to 6
- modulation: float32 [512, 2, 2, 3072], P('bag'), may hold values from -3 to 3
- head_weight: bfloat16 [2, 3072, 6144], P(None, None, 'seq'), may hold values from -0.109375 to 0.109375
- norm_gain: float32 [2, 2, 128], replicated, may hold values from 0.5 to 20
- store_down: bfloat16 [512, 2, 64, 3072], P('bag', None, 'seq'), may hold values from -0.109375 to 0.109375
- store_up: bfloat16 [512, 2, 64, 6144], P('bag', None, None, 'seq'), may hold values from -0.375 to 0.375
- store_row: int32 [512], replicated, may hold values from 0 to 511, as said below
- user_adapter: int32 [16, 16], replicated, may hold values from 0 to 511, as said below
- image_lengths: int32 [16, 16], P('bag'), may hold values from 1 to 128, 256 in all within a row
Outputs:
- text_out: bfloat16 [32768, 2048], P(('bag', 'seq'))
- image_out: bfloat16 [8192, 2048], P(('bag', 'seq'))
Inputs may be any that keep to these rules, and one draw needn't show every extreme that they name: A permutation: adapter a is kept at row store_row[a] of store_down and store_up, whose owner is store_row[a] // 32. `user_adapter`: the 16 users of one bag have adapters kept by 16 different owners, so every owner keeps exactly one adapter of each bag.
All inputs are finite; a program needn't handle non-finite values.
Results may differ from a plain program's by a relative error of at most 0.04.
The roundings to bfloat16 on the way count: a program that leaves them out, or rounds other values in their place, can miss the bound.
Values may be sent and summed in bfloat16 or wider, within the bound.
A program may use at most 128 MiB of HBM per device.

v0:
```python
import functools
import math

import jax
import jax.numpy as jnp
from jax import lax
from jax.experimental import pallas as pl
from jax.experimental.pallas import tpu as pltpu
from jax.sharding import PartitionSpec as P

MESH = pl.DeviceIdType.MESH
BF16 = jnp.bfloat16
F32 = jnp.float32
I32 = jnp.int32
HEAD_DIM = 128
TEXT = 64
NEG = -1e30
NT = (((1,), (1,)), ((), ()))
TN = (((0,), (0,)), ((), ()))


def iota(shape, axis):
    return lax.broadcasted_iota(I32, shape, axis)


def normed(values):
    centre = values - jnp.mean(values, axis=-1, keepdims=True)
    spread = jnp.mean(centre * centre, axis=-1, keepdims=True)
    return centre * lax.rsqrt(spread + 1e-06)


def head_normed(values, gain_row):
    spread = jnp.mean(values * values, axis=-1, keepdims=True)
    return (values * lax.rsqrt(spread + 1e-06) * gain_row).astype(BF16)


def dot(a, b):
    return jnp.dot(a, b, preferred_element_type=F32)


def dot_g(a, b, dims):
    return lax.dot_general(a, b, dims, preferred_element_type=F32)


def kernel(
    bags,
    ring,
    store_size,
    user_adapter,
    store_row,
    image_lengths,
    text_in,
    image_in,
    mod_in,
    weight_in,
    gain_in,
    down_in,
    up_in,
    text_out,
    image_out,
    own,
    slot,
    ends,
    text_raw,
    image_raw,
    mod,
    weight,
    gain,
    down_store,
    up_store,
    down_send,
    up_send,
    down_recv,
    up_recv,
    down_fwd,
    text_down,
    image_scale,
    text_all,
    image_all,
    rank_all,
    image_rank,
    seg_row,
    seg_col,
    own_col,
    query_image,
    key_image,
    value_image,
    key_text,
    value_text,
    text_stage,
    image_stage,
    local_sem,
    bag_send,
    bag_recv,
    seq_send,
    seq_recv,
    ring_send,
    ring_recv,
    mate_send,
    mate_recv,
):
    seqs = 2 * ring
    half_ring = ring // 2
    users = seqs
    bag = lax.axis_index("bag")
    seq = lax.axis_index("seq")
    z, core = seq // 2, lax.rem(seq, 2)
    mate = z * 2 + 1 - core
    depth = text_raw.shape[1]
    text_rows = text_raw.shape[0]
    image_rows = image_raw.shape[0]
    image_bag = seqs * image_rows
    image_half = image_rows // 2
    factor = 1.0 / math.sqrt(HEAD_DIM)

    pairs = (
        (image_in, image_raw),
        (mod_in, mod),
        (text_in, text_raw),
        (down_in, down_store),
        (up_in, up_store),
        (gain_in, gain),
        (weight_in, weight),
    )
    loads = [
        pltpu.make_async_copy(src, dst, local_sem.at[i]) for i, (src, dst) in enumerate(pairs)
    ]
    for load in loads:
        load.start()

    barrier = pltpu.get_barrier_semaphore()

    @pl.loop(1, seqs)
    def _(j):
        pl.semaphore_signal(
            barrier, inc=1, device_id={"seq": lax.rem(seq + j, seqs)}, device_id_type=MESH
        )

    @pl.loop(1, bags)
    def _(j):
        pl.semaphore_signal(
            barrier, inc=1, device_id={"bag": lax.rem(bag + j, bags)}, device_id_type=MESH
        )

    def end_step(u, before):
        length = image_lengths[0, u]
        ends[2 * u] = before + length
        ends[2 * u + 1] = before + 2 * length
        own[u] = store_row[user_adapter[bag, u]] // store_size
        return before + 2 * length

    lax.fori_loop(0, users, end_step, jnp.int32(0))

    @pl.loop(0, bags)
    def _(b):
        def one(u, total):
            row = store_row[user_adapter[b, u]]
            return total + jnp.where(row // store_size == bag, lax.rem(row, store_size), 0)

        slot[b] = lax.fori_loop(0, users, one, jnp.int32(0))

    row_ids = iota((1, image_bag), 1)
    col_ids = iota((image_bag, HEAD_DIM), 0)

    def seg_step(j, pair):
        end = ends[j]
        return (
            pair[0] + (row_ids >= end).astype(I32),
            pair[1] + (col_ids >= end).astype(I32),
        )

    seg_r, seg_c = lax.fori_loop(
        0, 2 * users, seg_step, (jnp.zeros_like(row_ids), jnp.zeros_like(col_ids))
    )
    seg_row[...] = seg_r
    seg_col[...] = seg_c

    def own_step(u, pair):
        owner = own[u]
        return (
            pair[0] + jnp.where(seg_r // 2 == u, owner, 0),
            pair[1] + jnp.where(seg_c // 2 == u, owner, 0),
        )

    own_r, own_c = lax.fori_loop(
        0, users, own_step, (jnp.zeros_like(row_ids), jnp.zeros_like(col_ids))
    )
    own_col[...] = own_c

    loads[0].wait()
    loads[1].wait()

    @pl.loop(0, image_rows)
    def _(i):
        row = seq * image_rows + i
        seg = lax.fori_loop(
            0, 2 * users, lambda j, n: n + (row >= ends[j]).astype(I32), jnp.int32(0)
        )
        seg = jnp.minimum(seg, 2 * users - 1)
        image_scale[0, pl.ds(i, 1), :] = mod[seg, 1, 0:1, :]
        image_scale[1, pl.ds(i, 1), :] = mod[seg, 1, 1:2, :]

    for half in range(2):
        part = pl.ds(half * image_half, image_half)
        values = normed(image_raw[part, :].astype(F32))
        image_all[seq, half] = (
            (1.0 + image_scale[1, part, :]) * values + image_scale[0, part, :]
        ).astype(BF16)

    pl.semaphore_wait(barrier, seqs - 1 + bags - 1)

    blocks = (image_all, text_all)

    def slot_of(k, which):
        return lax.rem(z + k, ring) * 2 + which

    def ring_copy(st, d, k, half):
        chunk = blocks[st].at[slot_of(k, core), half]
        turn = ring - 1 if d == 0 else 1
        peer = lax.rem(z + (1 if d == 0 else ring - 1), ring) * 2 + core
        return pltpu.make_async_remote_copy(
            src_ref=chunk,
            dst_ref=chunk,
            send_sem=ring_send.at[st, d, k, half],
            recv_sem=ring_recv.at[st, lax.rem(k + turn, ring), half],
            device_id={"seq": peer},
            device_id_type=MESH,
        )

    def ring_arrival(st, k, half):
        chunk = blocks[st].at[slot_of(k, core), half]
        return pltpu.make_async_remote_copy(
            src_ref=chunk,
            dst_ref=chunk,
            send_sem=ring_send.at[st, 0, k, half],
            recv_sem=ring_recv.at[st, k, half],
            device_id={"seq": mate},
            device_id_type=MESH,
        )

    def mate_copy(st, k, half, which):
        chunk = blocks[st].at[slot_of(k, which), half]
        return pltpu.make_async_remote_copy(
            src_ref=chunk,
            dst_ref=chunk,
            send_sem=mate_send.at[st, k, half],
            recv_sem=mate_recv.at[st, k, half],
            device_id={"seq": mate},
            device_id_type=MESH,
        )

    def start_own(st, half):
        ring_copy(st, half, 0, half).start()
        ring_copy(st, 1 - half, 0, half).start()
        mate_copy(st, 0, half, core).start()

    def hop(st, h):
        for d, half in ((0, 0), (1, 1), (0, 1), (1, 0)):
            k = ring - h if d == 0 else h
            ring_arrival(st, k, half).wait_recv()
            if d == half:
                ring_copy(st, d, k, half).start()
            else:

                @pl.when(h < half_ring - 1)
                def _():
                    ring_copy(st, d, k, half).start()

            mate_copy(st, k, half, core).start()

    def last_hop(st):
        for half in range(2):
            ring_arrival(st, half_ring, half).wait_recv()
            mate_copy(st, half_ring, half, core).start()

    start_own(0, 0)
    start_own(0, 1)

    def down_copy(j):
        b = lax.rem(bag + j, bags)
        return pltpu.make_async_remote_copy(
            src_ref=down_send.at[b],
            dst_ref=down_recv.at[bag],
            send_sem=bag_send.at[0, j],
            recv_sem=bag_recv.at[0, j],
            device_id={"bag": b},
            device_id_type=MESH,
        )

    def up_copy(j):
        b = lax.rem(bag + j, bags)
        return pltpu.make_async_remote_copy(
            src_ref=up_send.at[b],
            dst_ref=up_recv.at[bag],
            send_sem=bag_send.at[1, j],
            recv_sem=bag_recv.at[1, j],
            device_id={"bag": b},
            device_id_type=MESH,
        )

    def bag_arrival(which, j):
        ref = (down_recv, up_recv)[which].at[lax.rem(bag + bags - j, bags)]
        return pltpu.make_async_remote_copy(
            src_ref=ref,
            dst_ref=ref,
            send_sem=bag_send.at[which, j],
            recv_sem=bag_recv.at[which, j],
            device_id={"bag": lax.rem(bag + j, bags)},
            device_id_type=MESH,
        )

    loads[3].wait()

    @pl.loop(1, bags)
    def _(j):
        b = lax.rem(bag + j, bags)
        down_send[b] = down_store[slot[b]]
        down_copy(j).start()

    down_recv[bag] = down_store[slot[bag]]

    loads[2].wait()
    for half in range(2):
        seg = 2 * seq + half
        shift = mod[seg, 0, 0:1, :]
        scale = 1.0 + mod[seg, 0, 1:2, :]

        @pl.loop(0, TEXT // 16)
        def _(i):
            values = normed(text_raw[pl.ds(half * TEXT + i * 16, 16), :].astype(F32))
            text_all[seq, half, pl.ds(i * 16, 16), :] = (scale * values + shift).astype(BF16)

        start_own(1, half)

    loads[4].wait()

    @pl.loop(1, bags)
    def _(j):
        b = lax.rem(bag + j, bags)
        up_send[b] = up_store[slot[b]]
        up_copy(j).start()

    up_recv[bag] = up_store[slot[bag]]

    hop(0, 1)

    def seq_copy(which, j, src, dst):
        return pltpu.make_async_remote_copy(
            src_ref=src,
            dst_ref=dst,
            send_sem=seq_send.at[which, j],
            recv_sem=seq_recv.at[which, j],
            device_id={"seq": lax.rem(seq + j, seqs)},
            device_id_type=MESH,
        )

    def ahead(j):
        return lax.rem(seq + j, seqs)

    def behind(j):
        return lax.rem(seq + seqs - j, seqs)

    def fwd_copy(j):
        return seq_copy(0, j, down_fwd.at[ahead(j)], text_down.at[seq])

    @pl.loop(1, bags)
    def _(j):
        bag_arrival(0, j).wait_recv()

    @pl.loop(1, seqs)
    def _(j):
        u = ahead(j)
        down_fwd[u] = down_recv[own[u], 0]
        fwd_copy(j).start()

    text_down[seq] = down_recv[own[seq], 0]

    @pl.loop(2, half_ring)
    def _(h):
        hop(0, h)

    last_hop(0)

    @pl.loop(1, seqs)
    def _(j):
        seq_copy(0, j, down_fwd.at[ahead(j)], text_down.at[behind(j)]).wait_recv()

    parts = 8 * seqs

    def rank_sums(downs, rows_lo, rows_hi):
        low = dot_g(downs, rows_lo, NT)
        high = dot_g(downs, rows_hi, NT)
        even = lax.rem(iota(low.shape, 0), 2) == 0
        mixed = jnp.where(even, low, high)
        total = mixed + pltpu.roll(mixed, low.shape[0] - 1, 0)
        return total, even

    downs = text_down[...].reshape(parts, depth // 2)
    total, even = rank_sums(
        downs,
        text_all[seq, :, :, : depth // 2].reshape(text_rows, depth // 2),
        text_all[seq, :, :, depth // 2 :].reshape(text_rows, depth // 2),
    )
    sums = jnp.where(even, total, 0.0).astype(BF16)
    take = (iota((parts // 2, parts), 1) == 2 * iota((parts // 2, parts), 0)).astype(BF16)
    rank_all[seq] = dot(take, sums).astype(BF16)

    def rank_copy(j):
        return seq_copy(1, j, rank_all.at[seq], rank_all.at[seq])

    @pl.loop(1, seqs)
    def _(j):
        rank_copy(j).start()

    @pl.loop(0, ring)
    def _(k):
        for half in range(2):
            mate_copy(0, k, half, 1 - core).wait_recv()

    downs = down_recv[:, 1].reshape(8 * bags, depth // 2)
    total, even = rank_sums(
        downs,
        image_all[:, :, :, : depth // 2].reshape(image_bag, depth // 2),
        image_all[:, :, :, depth // 2 :].reshape(image_bag, depth // 2),
    )
    mine = jnp.logical_and(even, iota(total.shape, 0) // 8 == own_r)
    sums = jnp.where(mine, total, 0.0).astype(BF16)
    at = iota((8, 8 * bags), 0)
    take = jnp.logical_and(lax.rem(iota(at.shape, 1), 8) == 2 * at, at < 4)
    image_rank[seq] = dot(take.astype(BF16), sums).astype(BF16)

    def image_rank_copy(j):
        return seq_copy(2, j, image_rank.at[seq], image_rank.at[seq])

    @pl.loop(1, seqs)
    def _(j):
        image_rank_copy(j).start()

    @pl.loop(1, bags)
    def _(j):
        bag_arrival(1, j).wait_recv()

    @pl.loop(1, seqs)
    def _(j):
        ref = image_rank.at[behind(j)]
        seq_copy(2, j, ref, ref).wait_recv()

    loads[5].wait()
    loads[6].wait()
    rank = parts // 2
    up_image = up_recv[:, 1].reshape(bags * rank, 3 * HEAD_DIM)
    lane = lax.rem(iota((parts, bags * rank), 1), rank)
    copies = (iota((parts, bags * rank), 0) == 8 * (lane // 4) + lax.rem(lane, 4)).astype(BF16)
    ranks = image_rank[...].reshape(parts, image_bag)
    for lot in range(2):
        lo, rows = lot * image_bag // 2, image_bag // 2
        spread = dot_g(ranks[:, lo : lo + rows], copies, TN)
        here = iota(spread.shape, 1) // rank == own_col[lo : lo + rows, 0:1]
        spread = jnp.where(here, spread, 0.0).astype(BF16)
        lot_rows = image_all[lot * seqs // 2 : (lot + 1) * seqs // 2].reshape(rows, depth)
        mixed = dot(lot_rows, weight[1]) + dot(spread, up_image)
        query_image[lo : lo + rows] = head_normed(mixed[:, :HEAD_DIM], gain[1, 0:1])
        key_image[lo : lo + rows] = head_normed(
            mixed[:, HEAD_DIM : 2 * HEAD_DIM], gain[1, 1:2]
        )
        value_image[lo : lo + rows] = mixed[:, 2 * HEAD_DIM :].astype(BF16)

    def text_out_copy(j):
        return pltpu.make_async_remote_copy(
            src_ref=text_stage.at[ahead(j)],
            dst_ref=text_out.at[seq],
            send_sem=seq_send.at[3, j],
            recv_sem=seq_recv.at[3, j],
            device_id={"seq": ahead(j)},
            device_id_type=MESH,
        )

    def image_out_copy(j):
        return pltpu.make_async_remote_copy(
            src_ref=image_stage.at[ahead(j)],
            dst_ref=image_out.at[seq],
            send_sem=seq_send.at[4, j],
            recv_sem=seq_recv.at[4, j],
            device_id={"seq": ahead(j)},
            device_id_type=MESH,
        )

    text_local = pltpu.make_async_copy(text_stage.at[seq], text_out.at[seq], local_sem.at[7])
    image_local = pltpu.make_async_copy(image_stage.at[seq], image_out.at[seq], local_sem.at[8])

    @pl.loop(1, half_ring)
    def _(h):
        hop(1, h)

    last_hop(1)

    @pl.loop(0, ring)
    def _(k):
        for half in range(2):
            mate_copy(1, k, half, 1 - core).wait_recv()

    @pl.loop(1, seqs)
    def _(j):
        ref = rank_all.at[behind(j)]
        seq_copy(1, j, ref, ref).wait_recv()

    @pl.loop(0, ring)
    def _(p):
        odd = lax.rem(p, 2)
        k = odd * (ring - (p + 1) // 2) + (1 - odd) * (p // 2)
        first = slot_of(k, 0)
        rows = text_all[pl.ds(first, 2)].reshape(2 * text_rows, depth)
        plain = dot(rows, weight[0])
        image_segs = seg_row[...]
        for which in range(2):
            u = first + which
            j = lax.rem(seq + seqs - u, seqs)

            adjust = dot_g(rank_all[u], up_recv[own[u], 0], TN)
            mixed = plain[which * text_rows : (which + 1) * text_rows] + adjust
            query = head_normed(mixed[:, :HEAD_DIM], gain[0, 0:1])
            key = head_normed(mixed[:, HEAD_DIM : 2 * HEAD_DIM], gain[0, 1:2])
            value = mixed[:, 2 * HEAD_DIM :].astype(BF16)
            key_text[u] = key
            value_text[u] = value
            near = dot_g(query, key, NT) * factor
            same = iota(near.shape, 0) // TEXT == iota(near.shape, 1) // TEXT
            near = jnp.where(same, near, NEG)
            far = dot_g(query, key_image[...], NT) * factor
            same = 2 * u + iota(far.shape, 0) // TEXT == image_segs
            far = jnp.where(same, far, NEG)
            top = jnp.maximum(
                jnp.max(near, axis=1, keepdims=True), jnp.max(far, axis=1, keepdims=True)
            )
            near = jnp.exp(near - top)
            far = jnp.exp(far - top)
            total = jnp.sum(near, axis=1, keepdims=True) + jnp.sum(far, axis=1, keepdims=True)
            result = dot((near / total).astype(BF16), value) + dot(
                (far / total).astype(BF16), value_image[...]
            )
            text_stage[u] = result.astype(BF16)

            @pl.when(j != 0)
            def _():
                text_out_copy(lax.rem(u + seqs - seq, seqs)).start()

            @pl.when(j == 0)
            def _():
                text_local.start()

    keys = key_text[...].reshape(seqs * text_rows, HEAD_DIM)
    values = value_text[...].reshape(seqs * text_rows, HEAD_DIM)

    @pl.loop(0, image_bag // HEAD_DIM)
    def _(lot):
        part = pl.ds(lot * HEAD_DIM, HEAD_DIM)
        query = query_image[part, :]
        segs = seg_col[part, 0:1]
        near = dot_g(query, key_image[...], NT) * factor
        near = jnp.where(segs == seg_row[...], near, NEG)
        far = dot_g(query, keys, NT) * factor
        far = jnp.where(segs == iota(far.shape, 1) // TEXT, far, NEG)
        top = jnp.maximum(
            jnp.max(near, axis=1, keepdims=True), jnp.max(far, axis=1, keepdims=True)
        )
        near = jnp.exp(near - top)
        far = jnp.exp(far - top)
        total = jnp.sum(near, axis=1, keepdims=True) + jnp.sum(far, axis=1, keepdims=True)
        result = dot((near / total).astype(BF16), value_image[...]) + dot(
            (far / total).astype(BF16), values
        )
        per = HEAD_DIM // image_rows
        image_stage[pl.ds(lot * per, per)] = result.astype(BF16).reshape(
            per, image_rows, HEAD_DIM
        )

    image_local.start()

    @pl.loop(1, seqs)
    def _(j):
        image_out_copy(j).start()

    text_local.wait()
    image_local.wait()

    @pl.loop(1, seqs)
    def _(j):
        seq_copy(3, j, text_stage.at[seq], text_out.at[behind(j)]).wait_recv()
        seq_copy(4, j, image_stage.at[seq], image_out.at[behind(j)]).wait_recv()
        fwd_copy(j).wait_send()
        rank_copy(j).wait_send()
        image_rank_copy(j).wait_send()
        text_out_copy(j).wait_send()
        image_out_copy(j).wait_send()

    @pl.loop(1, bags)
    def _(j):
        down_copy(j).wait_send()
        up_copy(j).wait_send()

    @pl.loop(0, ring)
    def _(k):
        for st in range(2):
            for half in range(2):
                mate_copy(st, k, half, core).wait_send()

    @pl.loop(0, half_ring - 1)
    def _(h):
        for st in range(2):
            for half in range(2):
                ring_copy(st, 0, lax.rem(ring - h, ring), half).wait_send()
                ring_copy(st, 1, h, half).wait_send()

    for st in range(2):
        ring_copy(st, 0, half_ring + 1, 0).wait_send()
        ring_copy(st, 1, half_ring - 1, 1).wait_send()


def body(
    bags,
    seqs,
    text_rows,
    image_rows,
    modulation,
    head_weight,
    norm_gain,
    store_down,
    store_up,
    store_row,
    user_adapter,
    image_lengths,
):
    ring = seqs // 2
    text_dev, depth = text_rows.shape
    image_dev = image_rows.shape[0]
    image_bag = image_dev * seqs
    store_size = store_down.shape[0]
    rank, width = store_up.shape[2:]
    heads = seqs * HEAD_DIM
    store_down = store_down.reshape(store_size, 2, 8, depth // 2)
    smem = pl.BlockSpec(memory_space=pltpu.SMEM)
    hbm = pl.BlockSpec(memory_space=pl.ANY)
    vmem = pltpu.VMEM
    dma = pltpu.SemaphoreType.DMA
    text_heads, image_heads = pl.pallas_call(
        functools.partial(kernel, bags, ring, store_size),
        out_shape=(
            jax.ShapeDtypeStruct((seqs, text_dev, HEAD_DIM), BF16),
            jax.ShapeDtypeStruct((seqs, image_dev, HEAD_DIM), BF16),
        ),
        in_specs=[smem] * 3 + [hbm] * 7,
        out_specs=(hbm, hbm),
        scratch_shapes=[
            pltpu.SMEM((seqs,), I32),
            pltpu.SMEM((bags,), I32),
            pltpu.SMEM((2 * seqs,), I32),
            vmem((text_dev, depth), BF16),
            vmem((image_dev, depth), BF16),
            vmem(modulation.shape, F32),
            vmem(head_weight.shape, BF16),
            vmem(norm_gain.shape, F32),
            vmem(store_down.shape, BF16),
            vmem(store_up.shape, BF16),
            vmem((bags, 2, 8, depth // 2), BF16),
            vmem((bags, 2, rank, width), BF16),
            vmem((bags, 2, 8, depth // 2), BF16),
            vmem((bags, 2, rank, width), BF16),
            vmem((seqs, 8, depth // 2), BF16),
            vmem((seqs, 8, depth // 2), BF16),
            vmem((2, image_dev, depth), F32),
            vmem((seqs, 2, text_dev // 2, depth), BF16),
            vmem((seqs, 2, image_dev // 2, depth), BF16),
            vmem((seqs, rank, text_dev), BF16),
            vmem((seqs, 8, image_bag), BF16),
            vmem((1, image_bag), I32),
            vmem((image_bag, HEAD_DIM), I32),
            vmem((image_bag, HEAD_DIM), I32),
            vmem((image_bag, HEAD_DIM), BF16),
            vmem((image_bag, HEAD_DIM), BF16),
            vmem((image_bag, HEAD_DIM), BF16),
            vmem((seqs, text_dev, HEAD_DIM), BF16),
            vmem((seqs, text_dev, HEAD_DIM), BF16),
            vmem((seqs, text_dev, HEAD_DIM), BF16),
            vmem((seqs, image_dev, HEAD_DIM), BF16),
            dma((9,)),
            dma((2, bags)),
            dma((2, bags)),
            dma((5, seqs)),
            dma((5, seqs)),
            dma((2, 2, ring, 2)),
            dma((2, ring, 2)),
            dma((2, ring, 2)),
            dma((2, ring, 2)),
        ],
        compiler_params=pltpu.CompilerParams(
            collective_id=0, has_side_effects=True, vmem_limit_bytes=58 * 2**20
        ),
    )(
        user_adapter,
        store_row,
        image_lengths,
        text_rows,
        image_rows,
        modulation,
        head_weight,
        norm_gain,
        store_down,
        store_up,
    )
    return (
        jnp.transpose(text_heads, (1, 0, 2)).reshape(text_dev, heads),
        jnp.transpose(image_heads, (1, 0, 2)).reshape(image_dev, heads),
    )


def solution(mesh):
    in_specs = (
        P(("bag", "seq"), None),
        P(("bag", "seq"), None),
        P("bag", None, None, None),
        P(None, None, "seq"),
        P(),
        P("bag", None, "seq", None),
        P("bag", None, None, "seq"),
        P(),
        P(),
        P("bag", None),
    )
    out_specs = (P(("bag", "seq"), None), P(("bag", "seq"), None))
    return jax.shard_map(
        functools.partial(body, mesh.shape["bag"], mesh.shape["seq"]),
        mesh=mesh,
        in_specs=in_specs,
        out_specs=out_specs,
        check_vma=False,
    )
```

profile of v0, /device:TPU:1, one launch (start us, length us, event | category | flops | bytes accessed | tf_op | source)
XLA Modules:
  0.0 169.3 jit_solution(1413899625709812678)
XLA Ops:
  0.6 3.9 %reshape.13.down_in = bf16[32,2,8,1536]{3,2,1,0:T(8,128)(2,1)} reshape(bf16[32,2,4,3072]{3,2,1,0:T(4,128)(2,1)} %param.15) | data formatting | bytes 3145728 | tf_op jit(solution)/shard_map/reshape | solution.py:640
  4.5 161.8 %shard_map.113 = (bf16[16,128,128]{2,1,0:T(8,128)(2,1)}, bf16[16,32,128]{2,1,0:T(8,128)(2,1)}) custom-call(s32[16,16]{1,0:T(8,128)} %user_adapter.1, s32[512]{0:T(512)} %store_row.1, s32[1,16]{1,0:T(1,128)} %image_lengths.1, bf16[128,3072]{1,0:T(8,128)(2,1)} %text_in.1, bf16[32,3072]{1,0:T(8,128)(2,1)} %image_in.1, f32[32,2,2,3072]{3,2,1,0:T(2,128)} %mod_in.1, ...), custom_call_target="tpu_custom_call" | custom-call | tf_op jit(solution)/shard_map/pallas_call | solution.py:645
  166.3 0.0 copy-start
  166.3 1.3 copy.12
  167.7 1.0 copy.14
  168.7 0.0 copy-done
  168.7 0.7 copy_bitcast_fusion
Async XLA Ops:
  166.3 2.4 %copy-start = (bf16[16,32,128]{2,1,0:T(8,128)(2,1)S(1)}, bf16[16,32,128]{2,1,0:T(8,128)(2,1)}, u32[]{:S(2)}) copy-start(bf16[16,32,128]{2,1,0:T(8,128)(2,1)} %get-tuple-element.5) | copy-start | bytes 393220
where the time goes:
time: 172 us; the launch traced here: 169 us
  Pallas kernels  162 us (94%)
  local copies, waits for them, and re-layouts  6.88 us (4%)
    pallas_call x1, Pallas kernels, body(): pl.pallas_call(functools.partial(kernel, bags, ring, store_size), out_sha...  162 us
    reshape x1, local copies, waits for them, and re-layouts, body(): store_down = store_down.reshape(store_size, 2, 8, depth // 2)  3.85 us

commit v1 on v0

--- a/solution.py
+++ b/solution.py
@@ -102,6 +102,8 @@
     seqs = 2 * ring
     half_ring = ring // 2
     users = seqs
+    steps = [users >> i for i in range(users.bit_length())]
+    store_bits = store_size.bit_length() - 1
     bag = lax.axis_index("bag")
     seq = lax.axis_index("seq")
     z, core = seq // 2, lax.rem(seq, 2)
@@ -142,50 +144,12 @@
             barrier, inc=1, device_id={"bag": lax.rem(bag + j, bags)}, device_id_type=MESH
         )
 
-    def end_step(u, before):
+    before = jnp.int32(0)
+    for u in range(users):
         length = image_lengths[0, u]
         ends[2 * u] = before + length
-        ends[2 * u + 1] = before + 2 * length
-        own[u] = store_row[user_adapter[bag, u]] // store_size
-        return before + 2 * length
-
-    lax.fori_loop(0, users, end_step, jnp.int32(0))
-
-    @pl.loop(0, bags)
-    def _(b):
-        def one(u, total):
-            row = store_row[user_adapter[b, u]]
-            return total + jnp.where(row // store_size == bag, lax.rem(row, store_size), 0)
-
-        slot[b] = lax.fori_loop(0, users, one, jnp.int32(0))
-
-    row_ids = iota((1, image_bag), 1)
-    col_ids = iota((image_bag, HEAD_DIM), 0)
-
-    def seg_step(j, pair):
-        end = ends[j]
-        return (
-            pair[0] + (row_ids >= end).astype(I32),
-            pair[1] + (col_ids >= end).astype(I32),
-        )
-
-    seg_r, seg_c = lax.fori_loop(
-        0, 2 * users, seg_step, (jnp.zeros_like(row_ids), jnp.zeros_like(col_ids))
-    )
-    seg_row[...] = seg_r
-    seg_col[...] = seg_c
-
-    def own_step(u, pair):
-        owner = own[u]
-        return (
-            pair[0] + jnp.where(seg_r // 2 == u, owner, 0),
-            pair[1] + jnp.where(seg_c // 2 == u, owner, 0),
-        )
-
-    own_r, own_c = lax.fori_loop(
-        0, users, own_step, (jnp.zeros_like(row_ids), jnp.zeros_like(col_ids))
-    )
-    own_col[...] = own_c
+        before = before + 2 * length
+        ends[2 * u + 1] = before
 
     loads[0].wait()
     loads[1].wait()
@@ -193,10 +157,9 @@
     @pl.loop(0, image_rows)
     def _(i):
         row = seq * image_rows + i
-        seg = lax.fori_loop(
-            0, 2 * users, lambda j, n: n + (row >= ends[j]).astype(I32), jnp.int32(0)
-        )
-        seg = jnp.minimum(seg, 2 * users - 1)
+        seg = jnp.int32(0)
+        for step in steps:
+            seg = seg + jnp.where(row >= ends[seg + step - 1], step, 0)
         image_scale[0, pl.ds(i, 1), :] = mod[seg, 1, 0:1, :]
         image_scale[1, pl.ds(i, 1), :] = mod[seg, 1, 1:2, :]
 
@@ -309,15 +272,27 @@
             device_id_type=MESH,
         )
 
+    @pl.loop(0, bags)
+    def _(b):
+        total = jnp.int32(0)
+        for u in range(users):
+            row = store_row[user_adapter[b, u]]
+            total = total + jnp.where(row >> store_bits == bag, row & (store_size - 1), 0)
+        slot[b] = total
+
     loads[3].wait()
 
+    def put_down(ref, index, block):
+        ref[index, :, 0:4, :] = block[:, :, : depth // 2]
+        ref[index, :, 4:8, :] = block[:, :, depth // 2 :]
+
     @pl.loop(1, bags)
     def _(j):
         b = lax.rem(bag + j, bags)
-        down_send[b] = down_store[slot[b]]
+        put_down(down_send, b, down_store[slot[b]])
         down_copy(j).start()
 
-    down_recv[bag] = down_store[slot[bag]]
+    put_down(down_recv, bag, down_store[slot[bag]])
 
     loads[2].wait()
     for half in range(2):
@@ -342,6 +317,25 @@
 
     up_recv[bag] = up_store[slot[bag]]
 
+    row_ids = iota((1, image_bag), 1)
+    segs = jnp.zeros_like(row_ids)
+    owners = jnp.zeros_like(row_ids)
+    for j in range(2 * users):
+        segs = segs + (row_ids >= ends[j]).astype(I32)
+    for u in range(users):
+        owner = store_row[user_adapter[bag, u]] >> store_bits
+        own[u] = owner
+        owners = owners + jnp.where(segs >> 1 == u, owner, 0)
+    seg_row[...] = segs
+    own_r = owners
+
+    def as_column(row):
+        wide = jnp.broadcast_to(row.astype(F32), (HEAD_DIM, image_bag))
+        return jnp.transpose(wide).astype(I32)
+
+    seg_col[...] = as_column(segs)
+    own_col[...] = as_column(owners)
+
     hop(0, 1)
 
     def seq_copy(which, j, src, dst):
@@ -390,19 +384,20 @@
     def rank_sums(downs, rows_lo, rows_hi):
         low = dot_g(downs, rows_lo, NT)
         high = dot_g(downs, rows_hi, NT)
-        even = lax.rem(iota(low.shape, 0), 2) == 0
-        mixed = jnp.where(even, low, high)
-        total = mixed + pltpu.roll(mixed, low.shape[0] - 1, 0)
-        return total, even
+        first = iota(low.shape, 0) & 7 < 4
+        mixed = jnp.where(first, low, high)
+        total = mixed + pltpu.roll(mixed, low.shape[0] - 4, 0)
+        return total, first
 
     downs = text_down[...].reshape(parts, depth // 2)
-    total, even = rank_sums(
+    total, first = rank_sums(
         downs,
         text_all[seq, :, :, : depth // 2].reshape(text_rows, depth // 2),
         text_all[seq, :, :, depth // 2 :].reshape(text_rows, depth // 2),
     )
-    sums = jnp.where(even, total, 0.0).astype(BF16)
-    take = (iota((parts // 2, parts), 1) == 2 * iota((parts // 2, parts), 0)).astype(BF16)
+    sums = jnp.where(first, total, 0.0).astype(BF16)
+    at = iota((parts // 2, parts), 0)
+    take = (iota((parts // 2, parts), 1) == 8 * (at >> 2) + (at & 3)).astype(BF16)
     rank_all[seq] = dot(take, sums).astype(BF16)
 
     def rank_copy(j):
@@ -418,15 +413,15 @@
             mate_copy(0, k, half, 1 - core).wait_recv()
 
     downs = down_recv[:, 1].reshape(8 * bags, depth // 2)
-    total, even = rank_sums(
+    total, first = rank_sums(
         downs,
         image_all[:, :, :, : depth // 2].reshape(image_bag, depth // 2),
         image_all[:, :, :, depth // 2 :].reshape(image_bag, depth // 2),
     )
-    mine = jnp.logical_and(even, iota(total.shape, 0) // 8 == own_r)
+    mine = jnp.logical_and(first, iota(total.shape, 0) >> 3 == own_r)
     sums = jnp.where(mine, total, 0.0).astype(BF16)
     at = iota((8, 8 * bags), 0)
-    take = jnp.logical_and(lax.rem(iota(at.shape, 1), 8) == 2 * at, at < 4)
+    take = jnp.logical_and(iota(at.shape, 1) & 7 == at, at < 4)
     image_rank[seq] = dot(take.astype(BF16), sums).astype(BF16)
 
     def image_rank_copy(j):
@@ -449,13 +444,14 @@
     loads[6].wait()
     rank = parts // 2
     up_image = up_recv[:, 1].reshape(bags * rank, 3 * HEAD_DIM)
-    lane = lax.rem(iota((parts, bags * rank), 1), rank)
-    copies = (iota((parts, bags * rank), 0) == 8 * (lane // 4) + lax.rem(lane, 4)).astype(BF16)
+    rank_bits = rank.bit_length() - 1
+    lane = iota((parts, bags * rank), 1) & (rank - 1)
+    copies = (iota((parts, bags * rank), 0) == 8 * (lane >> 2) + (lane & 3)).astype(BF16)
     ranks = image_rank[...].reshape(parts, image_bag)
     for lot in range(2):
         lo, rows = lot * image_bag // 2, image_bag // 2
         spread = dot_g(ranks[:, lo : lo + rows], copies, TN)
-        here = iota(spread.shape, 1) // rank == own_col[lo : lo + rows, 0:1]
+        here = iota(spread.shape, 1) >> rank_bits == own_col[lo : lo + rows, 0:1]
         spread = jnp.where(here, spread, 0.0).astype(BF16)
         lot_rows = image_all[lot * seqs // 2 : (lot + 1) * seqs // 2].reshape(rows, depth)
         mixed = dot(lot_rows, weight[1]) + dot(spread, up_image)
@@ -524,10 +520,10 @@
             key_text[u] = key
             value_text[u] = value
             near = dot_g(query, key, NT) * factor
-            same = iota(near.shape, 0) // TEXT == iota(near.shape, 1) // TEXT
+            same = iota(near.shape, 0) >> 6 == iota(near.shape, 1) >> 6
             near = jnp.where(same, near, NEG)
             far = dot_g(query, key_image[...], NT) * factor
-            same = 2 * u + iota(far.shape, 0) // TEXT == image_segs
+            same = 2 * u + (iota(far.shape, 0) >> 6) == image_segs
             far = jnp.where(same, far, NEG)
             top = jnp.maximum(
                 jnp.max(near, axis=1, keepdims=True), jnp.max(far, axis=1, keepdims=True)
@@ -559,7 +555,7 @@
         near = dot_g(query, key_image[...], NT) * factor
         near = jnp.where(segs == seg_row[...], near, NEG)
         far = dot_g(query, keys, NT) * factor
-        far = jnp.where(segs == iota(far.shape, 1) // TEXT, far, NEG)
+        far = jnp.where(segs == iota(far.shape, 1) >> 6, far, NEG)
         top = jnp.maximum(
             jnp.max(near, axis=1, keepdims=True), jnp.max(far, axis=1, keepdims=True)
         )
@@ -637,7 +633,6 @@
     store_size = store_down.shape[0]
     rank, width = store_up.shape[2:]
     heads = seqs * HEAD_DIM
-    store_down = store_down.reshape(store_size, 2, 8, depth // 2)
     smem = pl.BlockSpec(memory_space=pltpu.SMEM)
     hbm = pl.BlockSpec(memory_space=pl.ANY)
     vmem = pltpu.VMEM

time: 172 us -> 154 us (0.90); the launches traced: 169 us -> 153 us
  Pallas kernels: 162 us -> 149 us
  local copies, waits for them, and re-layouts: 6.88 us -> 3.89 us
    pallas_call x1, Pallas kernels: 162 us -> 149 us  [body(): pl.pallas_call(functools.partial(kernel, bags, ring, store_size), out_sha...]
    reshape x1 -> x0, local copies, waits for them, and re-layouts: 3.85 us -> none  [body(): store_down = store_down.reshape(store_size, 2, 8, depth // 2)]
where the time goes in v1:
time: 154 us; the launch traced here: 153 us
  Pallas kernels  149 us (97%)
  local copies, waits for them, and re-layouts  3.89 us (3%)
    pallas_call x1, Pallas kernels, body(): pl.pallas_call(functools.partial(kernel, bags, ring, store_size), out_sha...  149 us

profile of v1, /device:TPU:1, one launch (start us, length us, event | category | flops | bytes accessed | tf_op | source)
XLA Modules:
  0.0 153.4 jit_solution(18389017093627327608)
XLA Ops:
  0.6 148.9 %shard_map.113 = (bf16[16,128,128]{2,1,0:T(8,128)(2,1)}, bf16[16,32,128]{2,1,0:T(8,128)(2,1)}) custom-call(s32[16,16]{1,0:T(8,128)} %user_adapter.1, s32[512]{0:T(512)} %store_row.1, s32[1,16]{1,0:T(1,128)} %image_lengths.1, bf16[128,3072]{1,0:T(8,128)(2,1)} %text_in.1, bf16[32,3072]{1,0:T(8,128)(2,1)} %image_in.1, f32[32,2,2,3072]{3,2,1,0:T(2,128)} %mod_in.1, ...), custom_call_target="tpu_custom_call" | custom-call | tf_op jit(solution)/shard_map/pallas_call | solution.py:640
  149.5 1.3 copy.12
  150.8 1.0 copy.14
  151.8 1.6 %copy_bitcast_fusion = bf16[32,2048]{1,0:T(8,128)(2,1)} fusion(bf16[16,32,128]{2,1,0:T(8,128)(2,1)} %get-tuple-element.5), kind=kLoop, calls=%fused_computation | loop fusion | bytes 262144 | tf_op jit(solution)/shard_map/reshape | solution.py:707

commit v2 on v1

--- a/solution.py
+++ b/solution.py
@@ -223,11 +223,8 @@
             ring_arrival(st, k, half).wait_recv()
             if d == half:
                 ring_copy(st, d, k, half).start()
-            else:
-
-                @pl.when(h < half_ring - 1)
-                def _():
-                    ring_copy(st, d, k, half).start()
+            elif h < half_ring - 1:
+                ring_copy(st, d, k, half).start()
 
             mate_copy(st, k, half, core).start()
 
@@ -369,11 +366,11 @@
 
     text_down[seq] = down_recv[own[seq], 0]
 
-    @pl.loop(2, half_ring)
-    def _(h):
+    for h in range(2, half_ring):
         hop(0, h)
-
     last_hop(0)
+
+    hop(1, 1)
 
     @pl.loop(1, seqs)
     def _(j):
@@ -400,12 +397,59 @@
     take = (iota((parts // 2, parts), 1) == 8 * (at >> 2) + (at & 3)).astype(BF16)
     rank_all[seq] = dot(take, sums).astype(BF16)
 
-    def rank_copy(j):
-        return seq_copy(1, j, rank_all.at[seq], rank_all.at[seq])
-
-    @pl.loop(1, seqs)
-    def _(j):
-        rank_copy(j).start()
+    rank_refs = (None, rank_all, image_rank)
+
+    def core_copy(which, j):
+        ref = rank_refs[which].at[seq]
+        return pltpu.make_async_remote_copy(
+            src_ref=ref,
+            dst_ref=ref,
+            send_sem=seq_send.at[which, j],
+            recv_sem=seq_recv.at[which, j],
+            device_id={"seq": slot_of(j, core)},
+            device_id_type=MESH,
+        )
+
+    def core_arrival(which, j):
+        ref = rank_refs[which].at[slot_of(ring - j, core)]
+        return pltpu.make_async_remote_copy(
+            src_ref=ref,
+            dst_ref=ref,
+            send_sem=seq_send.at[which, j],
+            recv_sem=seq_recv.at[which, j],
+            device_id={"seq": mate},
+            device_id_type=MESH,
+        )
+
+    def pass_copy(which, k, side):
+        ref = rank_refs[which].at[slot_of(k, side)]
+        return pltpu.make_async_remote_copy(
+            src_ref=ref,
+            dst_ref=ref,
+            send_sem=seq_send.at[which, ring + k],
+            recv_sem=seq_recv.at[which, ring + k],
+            device_id={"seq": mate},
+            device_id_type=MESH,
+        )
+
+    def send_ranks(which):
+        @pl.loop(1, ring)
+        def _(j):
+            core_copy(which, j).start()
+
+        pass_copy(which, 0, core).start()
+
+    def take_ranks(which):
+        @pl.loop(1, ring)
+        def _(j):
+            core_arrival(which, j).wait_recv()
+            pass_copy(which, ring - j, core).start()
+
+        @pl.loop(0, ring)
+        def _(k):
+            pass_copy(which, k, 1 - core).wait_recv()
+
+    send_ranks(1)
 
     @pl.loop(0, ring)
     def _(k):
@@ -424,22 +468,14 @@
     take = jnp.logical_and(iota(at.shape, 1) & 7 == at, at < 4)
     image_rank[seq] = dot(take.astype(BF16), sums).astype(BF16)
 
-    def image_rank_copy(j):
-        return seq_copy(2, j, image_rank.at[seq], image_rank.at[seq])
-
-    @pl.loop(1, seqs)
-    def _(j):
-        image_rank_copy(j).start()
+    send_ranks(2)
+    hop(1, 2)
 
     @pl.loop(1, bags)
     def _(j):
         bag_arrival(1, j).wait_recv()
 
-    @pl.loop(1, seqs)
-    def _(j):
-        ref = image_rank.at[behind(j)]
-        seq_copy(2, j, ref, ref).wait_recv()
-
+    take_ranks(2)
     loads[5].wait()
     loads[6].wait()
     rank = parts // 2
@@ -461,6 +497,9 @@
         )
         value_image[lo : lo + rows] = mixed[:, 2 * HEAD_DIM :].astype(BF16)
 
+    hop(1, 3)
+    take_ranks(1)
+
     def text_out_copy(j):
         return pltpu.make_async_remote_copy(
             src_ref=text_stage.at[ahead(j)],
@@ -484,21 +523,12 @@
     text_local = pltpu.make_async_copy(text_stage.at[seq], text_out.at[seq], local_sem.at[7])
     image_local = pltpu.make_async_copy(image_stage.at[seq], image_out.at[seq], local_sem.at[8])
 
-    @pl.loop(1, half_ring)
-    def _(h):
-        hop(1, h)
-
     last_hop(1)
 
     @pl.loop(0, ring)
     def _(k):
         for half in range(2):
             mate_copy(1, k, half, 1 - core).wait_recv()
-
-    @pl.loop(1, seqs)
-    def _(j):
-        ref = rank_all.at[behind(j)]
-        seq_copy(1, j, ref, ref).wait_recv()
 
     @pl.loop(0, ring)
     def _(p):
@@ -584,10 +614,18 @@
         seq_copy(3, j, text_stage.at[seq], text_out.at[behind(j)]).wait_recv()
         seq_copy(4, j, image_stage.at[seq], image_out.at[behind(j)]).wait_recv()
         fwd_copy(j).wait_send()
-        rank_copy(j).wait_send()
-        image_rank_copy(j).wait_send()
         text_out_copy(j).wait_send()
         image_out_copy(j).wait_send()
+
+    for which in (1, 2):
+
+        @pl.loop(1, ring)
+        def _(j):
+            core_copy(which, j).wait_send()
+
+        @pl.loop(0, ring)
+        def _(k):
+            pass_copy(which, k, core).wait_send()
 
     @pl.loop(1, bags)
     def _(j):

time: 154 us -> 142 us (0.922)
  Pallas kernels: 149 us -> 137 us
    pallas_call x1, Pallas kernels: 149 us -> 137 us  [body(): pl.pallas_call(functools.partial(kernel, bags, ring, store_size), out_sha...]
where the time goes in v2:
time: 142 us; the launch traced here: 141 us
  Pallas kernels  137 us (96%)
  local copies, waits for them, and re-layouts  3.89 us (3%)
    pallas_call x1, Pallas kernels, body(): pl.pallas_call(functools.partial(kernel, bags, ring, store_size), out_sha...  137 us

profile of v2, /device:TPU:1, one launch (start us, length us, event | category | flops | bytes accessed | tf_op | source)
XLA Modules:
  0.0 141.4 jit_solution(13017875306623223213)
XLA Ops:
  0.6 136.9 %shard_map.113 = (bf16[16,128,128]{2,1,0:T(8,128)(2,1)}, bf16[16,32,128]{2,1,0:T(8,128)(2,1)}) custom-call(s32[16,16]{1,0:T(8,128)} %user_adapter.1, s32[512]{0:T(512)} %store_row.1, s32[1,16]{1,0:T(1,128)} %image_lengths.1, bf16[128,3072]{1,0:T(8,128)(2,1)} %text_in.1, bf16[32,3072]{1,0:T(8,128)(2,1)} %image_in.1, f32[32,2,2,3072]{3,2,1,0:T(2,128)} %mod_in.1, ...), custom_call_target="tpu_custom_call" | custom-call | tf_op jit(solution)/shard_map/pallas_call | solution.py:678
  137.5 1.3 copy.12
  138.8 1.0 copy.14
  139.8 1.6 %copy_bitcast_fusion = bf16[32,2048]{1,0:T(8,128)(2,1)} fusion(bf16[16,32,128]{2,1,0:T(8,128)(2,1)} %get-tuple-element.5), kind=kLoop, calls=%fused_computation | loop fusion | bytes 262144 | tf_op jit(solution)/shard_map/reshape | solution.py:745

commit v3 on v2

--- a/solution.py
+++ b/solution.py
@@ -302,7 +302,6 @@
             values = normed(text_raw[pl.ds(half * TEXT + i * 16, 16), :].astype(F32))
             text_all[seq, half, pl.ds(i * 16, 16), :] = (scale * values + shift).astype(BF16)
 
-        start_own(1, half)
 
     loads[4].wait()
 
@@ -334,6 +333,10 @@
     own_col[...] = as_column(owners)
 
     hop(0, 1)
+    hop(0, 2)
+    start_own(1, 0)
+    start_own(1, 1)
+    hop(0, 3)
 
     def seq_copy(which, j, src, dst):
         return pltpu.make_async_remote_copy(
@@ -366,11 +369,8 @@
 
     text_down[seq] = down_recv[own[seq], 0]
 
-    for h in range(2, half_ring):
-        hop(0, h)
+    hop(1, 1)
     last_hop(0)
-
-    hop(1, 1)
 
     @pl.loop(1, seqs)
     def _(j):
@@ -500,6 +500,8 @@
     hop(1, 3)
     take_ranks(1)
 
+    group = 4
+
     def text_out_copy(j):
         return pltpu.make_async_remote_copy(
             src_ref=text_stage.at[ahead(j)],
@@ -530,15 +532,13 @@
         for half in range(2):
             mate_copy(1, k, half, 1 - core).wait_recv()
 
-    @pl.loop(0, ring)
+    @pl.loop(0, seqs // group)
     def _(p):
-        odd = lax.rem(p, 2)
-        k = odd * (ring - (p + 1) // 2) + (1 - odd) * (p // 2)
-        first = slot_of(k, 0)
-        rows = text_all[pl.ds(first, 2)].reshape(2 * text_rows, depth)
+        first = group * lax.rem(seq // group + p, seqs // group)
+        rows = text_all[pl.ds(first, group)].reshape(group * text_rows, depth)
         plain = dot(rows, weight[0])
         image_segs = seg_row[...]
-        for which in range(2):
+        for which in range(group):
             u = first + which
             j = lax.rem(seq + seqs - u, seqs)
 

time: 142 us -> 141 us (level)
  no operation moved by 1% of the time
where the time goes in v3:
time: 141 us
  Pallas kernels  136 us (96%)
  local copies, waits for them, and re-layouts  3.89 us (3%)
    pallas_call x1, Pallas kernels, body(): pl.pallas_call(functools.partial(kernel, bags, ring, store_size), out_sha...  136 us

profile of v3, /device:TPU:1, one launch (start us, length us, event | category | flops | bytes accessed | tf_op | source)
XLA Modules:
  0.0 140.9 jit_solution(11423650131712497037)
XLA Ops:
  0.6 136.4 %shard_map.113 = (bf16[16,128,128]{2,1,0:T(8,128)(2,1)}, bf16[16,32,128]{2,1,0:T(8,128)(2,1)}) custom-call(s32[16,16]{1,0:T(8,128)} %user_adapter.1, s32[512]{0:T(512)} %store_row.1, s32[1,16]{1,0:T(1,128)} %image_lengths.1, bf16[128,3072]{1,0:T(8,128)(2,1)} %text_in.1, bf16[32,3072]{1,0:T(8,128)(2,1)} %image_in.1, f32[32,2,2,3072]{3,2,1,0:T(2,128)} %mod_in.1, ...), custom_call_target="tpu_custom_call" | custom-call | tf_op jit(solution)/shard_map/pallas_call | solution.py:678
  137.0 1.3 copy.12
  138.4 1.0 copy.14
  139.4 1.6 %copy_bitcast_fusion = bf16[32,2048]{1,0:T(8,128)(2,1)} fusion(bf16[16,32,128]{2,1,0:T(8,128)(2,1)} %get-tuple-element.5), kind=kLoop, calls=%fused_computation | loop fusion | bytes 262144 | tf_op jit(solution)/shard_map/reshape | solution.py:745

commit v4 on v3

--- a/solution.py
+++ b/solution.py
@@ -113,7 +113,7 @@
     image_rows = image_raw.shape[0]
     image_bag = seqs * image_rows
     image_half = image_rows // 2
-    factor = 1.0 / math.sqrt(HEAD_DIM)
+    factor = math.log2(math.e) / math.sqrt(HEAD_DIM)
 
     pairs = (
         (image_in, image_raw),
@@ -470,6 +470,7 @@
 
     send_ranks(2)
     hop(1, 2)
+    hop(1, 3)
 
     @pl.loop(1, bags)
     def _(j):
@@ -497,7 +498,6 @@
         )
         value_image[lo : lo + rows] = mixed[:, 2 * HEAD_DIM :].astype(BF16)
 
-    hop(1, 3)
     take_ranks(1)
 
     group = 4
@@ -549,20 +549,21 @@
             value = mixed[:, 2 * HEAD_DIM :].astype(BF16)
             key_text[u] = key
             value_text[u] = value
-            near = dot_g(query, key, NT) * factor
+            near = dot_g(query, key, NT)
             same = iota(near.shape, 0) >> 6 == iota(near.shape, 1) >> 6
             near = jnp.where(same, near, NEG)
-            far = dot_g(query, key_image[...], NT) * factor
+            far = dot_g(query, key_image[...], NT)
             same = 2 * u + (iota(far.shape, 0) >> 6) == image_segs
             far = jnp.where(same, far, NEG)
             top = jnp.maximum(
                 jnp.max(near, axis=1, keepdims=True), jnp.max(far, axis=1, keepdims=True)
             )
-            near = jnp.exp(near - top)
-            far = jnp.exp(far - top)
+            near = jnp.exp2((near - top) * factor)
+            far = jnp.exp2((far - top) * factor)
             total = jnp.sum(near, axis=1, keepdims=True) + jnp.sum(far, axis=1, keepdims=True)
-            result = dot((near / total).astype(BF16), value) + dot(
-                (far / total).astype(BF16), value_image[...]
+            total = 1.0 / total
+            result = dot((near * total).astype(BF16), value) + dot(
+                (far * total).astype(BF16), value_image[...]
             )
             text_stage[u] = result.astype(BF16)
 
@@ -582,18 +583,19 @@
         part = pl.ds(lot * HEAD_DIM, HEAD_DIM)
         query = query_image[part, :]
         segs = seg_col[part, 0:1]
-        near = dot_g(query, key_image[...], NT) * factor
+        near = dot_g(query, key_image[...], NT)
         near = jnp.where(segs == seg_row[...], near, NEG)
-        far = dot_g(query, keys, NT) * factor
+        far = dot_g(query, keys, NT)
         far = jnp.where(segs == iota(far.shape, 1) >> 6, far, NEG)
         top = jnp.maximum(
             jnp.max(near, axis=1, keepdims=True), jnp.max(far, axis=1, keepdims=True)
         )
-        near = jnp.exp(near - top)
-        far = jnp.exp(far - top)
+        near = jnp.exp2((near - top) * factor)
+        far = jnp.exp2((far - top) * factor)
         total = jnp.sum(near, axis=1, keepdims=True) + jnp.sum(far, axis=1, keepdims=True)
-        result = dot((near / total).astype(BF16), value_image[...]) + dot(
-            (far / total).astype(BF16), values
+        total = 1.0 / total
+        result = dot((near * total).astype(BF16), value_image[...]) + dot(
+            (far * total).astype(BF16), values
         )
         per = HEAD_DIM // image_rows
         image_stage[pl.ds(lot * per, per)] = result.astype(BF16).reshape(

time: 141 us -> 141 us (level)
  no operation moved by 1% of the time
where the time goes in v4:
time: 141 us
  Pallas kernels  136 us (96%)
  local copies, waits for them, and re-layouts  3.89 us (3%)
    pallas_call x1, Pallas kernels, body(): pl.pallas_call(functools.partial(kernel, bags, ring, store_size), out_sha...  136 us

profile of v4, /device:TPU:1, one launch (start us, length us, event | category | flops | bytes accessed | tf_op | source)
XLA Modules:
  0.0 140.7 jit_solution(1541000229088871520)
XLA Ops:
  0.6 136.2 %shard_map.113 = (bf16[16,128,128]{2,1,0:T(8,128)(2,1)}, bf16[16,32,128]{2,1,0:T(8,128)(2,1)}) custom-call(s32[16,16]{1,0:T(8,128)} %user_adapter.1, s32[512]{0:T(512)} %store_row.1, s32[1,16]{1,0:T(1,128)} %image_lengths.1, bf16[128,3072]{1,0:T(8,128)(2,1)} %text_in.1, bf16[32,3072]{1,0:T(8,128)(2,1)} %image_in.1, f32[32,2,2,3072]{3,2,1,0:T(2,128)} %mod_in.1, ...), custom_call_target="tpu_custom_call" | custom-call | tf_op jit(solution)/shard_map/pallas_call | solution.py:680
  136.8 1.3 copy.12
  138.2 1.0 copy.14
  139.2 1.6 %copy_bitcast_fusion = bf16[32,2048]{1,0:T(8,128)(2,1)} fusion(bf16[16,32,128]{2,1,0:T(8,128)(2,1)} %get-tuple-element.5), kind=kLoop, calls=%fused_computation | loop fusion | bytes 262144 | tf_op jit(solution)/shard_map/reshape | solution.py:747
